TPU v7x, 32 devices: a whole 2x2x4 slice. The times are simulated.
32 devices in a mesh: grp: 4 (over z), inner: 8 (over y, x, core).
Axes of the slice: x: 2, y: 2, z: 4, core: 2. Of those that a mesh axis runs over, the one named last changes fastest.
Arguments:
- design: float32 [8, 4096, 1024], P('inner', 'grp'), may hold values from -6 to 6
- row_signs: int32 [8, 4096], P('inner', 'grp'), may hold values from 0 to 1
- kept_rows: int32 [8, 2048], P('inner'), may hold values from 0 to 4095, as said below
Outputs:
- factored: float32 [2048, 1024], P('grp')
Inputs may be any that keep to these rules, and one draw needn't show every extreme that they name: `kept_rows`: within each block the 2048 kept row numbers are distinct, and each block keeps its first and its last row.
All inputs are finite; a program needn't handle non-finite values.
Results may differ from a plain program's by a relative error of at most 0.0048.
Values may be sent and summed in bfloat16 or wider, within the bound.
No kernel may reach another device: no remote copies, remote signals or barrier semaphores. Data moves between devices by JAX's collectives and lax.ppermute only.
A program may use at most 64 MiB of HBM per device.

v0:
```python
import math
import jax
import jax.numpy as jnp
from jax import lax
from jax.sharding import PartitionSpec as P

COLS_DONE = 8
epsilon = 1e-06


def sign_table(row_ids, col_ids):
    common_bits = jnp.bitwise_and(row_ids[:, None], col_ids[None, :])
    ones_total = jnp.zeros(common_bits.shape, jnp.int32)
    for bit_pos in range(4):
        ones_total = ones_total + jnp.bitwise_and(jnp.right_shift(common_bits, bit_pos), 1)
    return 1.0 - 2.0 * jnp.bitwise_and(ones_total, 1).astype(jnp.float32)


def pick_rows(table_rows, chosen_rows):
    return jnp.take(table_rows, chosen_rows, axis=0)


def on_device(design, row_signs, kept_rows):
    block_count, local_rows, columns = design.shape
    keep_count = kept_rows.shape[1]
    groups = lax.axis_size("grp")
    owned_rows = keep_count // groups
    highest = lax.Precision.HIGHEST
    sixteen = jnp.arange(16, dtype=jnp.int32)
    hadamard = sign_table(sixteen, sixteen).astype(jnp.bfloat16)
    flipped = (design * (1 - 2 * row_signs).astype(jnp.float32)[:, :, None]).astype(jnp.bfloat16)
    lowest = flipped.reshape(block_count * local_rows // 16, 16, columns)
    first_pass = jnp.einsum(
        "hc,ncd->nhd", hadamard, lowest, preferred_element_type=jnp.float32
    ).astype(jnp.bfloat16)
    middle_view = first_pass.reshape(block_count * local_rows // 256, 16, 16, columns)
    second_pass = jnp.einsum(
        "hb,mbcd->mhcd", hadamard, middle_view, preferred_element_type=jnp.float32
    ).astype(jnp.bfloat16)
    second_pass = second_pass.reshape(block_count, local_rows, columns)
    gathered_rows = lax.all_to_all(second_pass, "grp", split_axis=2, concat_axis=1, tiled=True)
    col_count = gathered_rows.shape[2]
    by_piece = gathered_rows.reshape(block_count, 16, 256, col_count)
    mixed_rows = jnp.einsum("ha,nakd->nhkd", hadamard, by_piece, preferred_element_type=jnp.float32)
    mixed_rows = mixed_rows.reshape(block_count, 16 * 256, col_count)
    picked = jax.vmap(pick_rows)(mixed_rows, kept_rows)
    partial_value = jnp.sum(picked, axis=0)
    summed = lax.psum(partial_value, "inner")
    sketch = lax.all_to_all(summed, "grp", split_axis=0, concat_axis=1, tiled=True)
    sketch = sketch * (1.0 / (64.0 * math.sqrt(keep_count)))
    row_base = lax.axis_index("grp") * owned_rows
    global_rows = row_base + jnp.arange(owned_rows, dtype=jnp.int32)

    def reflect(col_index, current):
        column = jnp.where(global_rows >= col_index, current[:, col_index], 0.0)
        is_pivot = (global_rows == col_index).astype(jnp.float32)
        norm_sq, crossed, pivot_row = lax.psum(
            (
                jnp.sum(column * column),
                jnp.dot(column, current, precision=highest),
                jnp.dot(is_pivot, current, precision=highest),
            ),
            "grp",
        )
        pivot_value = pivot_row[col_index]
        head_value = -jnp.where(pivot_value >= 0, 1.0, -1.0) * jnp.sqrt(norm_sq)
        length = 2.0 * (norm_sq - head_value * pivot_value) + epsilon
        projected_row = crossed - head_value * pivot_row
        vector = column - head_value * is_pivot
        return current - vector[:, None] * (2.0 * projected_row / length)[None, :]

    result = lax.fori_loop(0, COLS_DONE, reflect, sketch)
    return result


def solution(mesh):
    return jax.shard_map(
        on_device,
        mesh=mesh,
        in_specs=(P("inner", "grp", None), P("inner", "grp"), P("inner", None)),
        out_specs=P("grp", None),
        check_vma=False,
    )
```

profile of v0, /device:TPU:0, one launch (start us, length us, event | category | flops | bytes accessed | tf_op | source)
XLA Modules:
  0.0 397.2 jit_solution(10092679646443896874)
XLA Ops:
  7.2 2.5 multiply_convert_fusion
  13.1 7.7 %copy.22 = bf16[1,1024,1024]{1,0,2:T(2,128)(2,1)} copy(bf16[1,1024,1024]{2,1,0:T(8,128)(2,1)S(1)} %bitcast.77) | data formatting | bytes 4194304 | tf_op jit(solution)/shard_map/reshape | solution.py:40
  21.4 12.8 %reduce.2 = bf16[1024,1024]{1,0:T(8,128)(2,1)S(1)} reduce(bf16[1024,1,1024]{2,1,0:T(2,128)(2,1)} %bitcast.75, bf16[]{:T(256)} %broadcast.106), dimensions={1}, to_apply=%bitcast.43.reduce_sub_computation | reduce | bytes 4194306
  34.2 2.8 reshape.93
  36.9 6.5 %all-to-all-start = ((bf16[4,2,131072]{2,1,0:T(2,128)(2,1)}), bf16[4,2,131072]{2,1,0:T(2,128)(2,1)S(1)}, u32[]{:S(2)}, u32[]{:S(2)}) async-start(bf16[4,2,131072]{2,1,0:T(2,128)(2,1)} %reshape.93), calls=%async_computation | async-start | bytes 4194304 | tf_op jit(solution)/shard_map/all_to_all | solution.py:41
  43.5 48.1 %all-to-all-done = bf16[4,2,131072]{2,1,0:T(2,128)(2,1)S(1)} async-done(((bf16[4,2,131072]{2,1,0:T(2,128)(2,1)}), bf16[4,2,131072]{2,1,0:T(2,128)(2,1)S(1)}, u32[]{:S(2)}, u32[]{:S(2)}) %all-to-all-start) | async-done | bytes 2097184 | tf_op jit(solution)/shard_map/all_to_all | solution.py:41
  91.6 3.4 reshape.94
  94.9 3.0 copy.29
  97.9 2.6 copy.23
  100.5 2.9 convolution_bitcast_fusion
  103.4 4.4 %copy.25 = f32[1,16,256,256]{3,2,1,0:T(8,128)} copy(f32[1,16,256,256]{3,1,2,0:T(8,128)S(1)} %convolution_bitcast_fusion) | data formatting | bytes 8388608 | tf_op jit(solution)/shard_map/ha,nakd->nhkd/transpose | solution.py:44
  107.8 21.4 %gather_fusion = f32[2048,256]{1,0:T(8,128)S(1)} fusion(f32[1,4096,256]{2,1,0:T(8,128)} %bitcast.74, s32[2048]{0:T(1024)S(1)} %bitcast.73), kind=kCustom, calls=%fused_computation | custom fusion | bytes 4210688 | tf_op jit(solution)/shard_map/vmap(jit(_take))/gather | solution.py:20
  130.8 61.1 %all-reduce.5.cloned.1.call-done = f32[4,512,256]{2,1,0:T(8,128)} async-done(((f32[4,512,256]{2,1,0:T(8,128)}), f32[4,512,256]{2,1,0:T(8,128)}) %all-reduce.5.cloned.1.call-update) | async-done | bytes 2097168 | tf_op jit(solution)/shard_map/psum | solution.py:48
  191.9 4.5 %all-to-all-start.1 = ((f32[4,512,256]{2,1,0:T(8,128)}), f32[4,512,256]{2,1,0:T(8,128)S(1)}, u32[]{:S(2)}, u32[]{:S(2)}) async-start(f32[4,512,256]{2,1,0:T(8,128)} %all-reduce.5.cloned.1.call-done), calls=%async_computation.1 | async-start | bytes 4194304 | tf_op jit(solution)/shard_map/all_to_all | solution.py:49
  196.4 47.1 %all-to-all-done.1 = f32[4,512,256]{2,1,0:T(8,128)S(1)} async-done(((f32[4,512,256]{2,1,0:T(8,128)}), f32[4,512,256]{2,1,0:T(8,128)S(1)}, u32[]{:S(2)}, u32[]{:S(2)}) %all-to-all-start.1) | async-done | bytes 2097184 | tf_op jit(solution)/shard_map/all_to_all | solution.py:49
  245.1 1.9 copy.26
  247.0 141.5 %while.14 = (s32[]{:T(128)}, f32[512,1024]{0,1:T(8,128)S(1)}, s32[]{:T(128)}, s32[]{:T(128)}, f32[]{:T(128)}, /*index=5*/f32[]{:T(128)}, f32[]{:T(128)}, f32[]{:T(128)}, f32[]{:T(128)}) while((s32[]{:T(128)}, f32[512,1024]{0,1:T(8,128)S(1)}, s32[]{:T(128)}, s32[]{:T(128)}, f32[]{:T(128)}, /*index=5*/f32[]{:T(128)}, f32[]{:T(128)}, ...), condition=%wide.region_6.7_spmd.clone, body=%wide.region_1.6_spmd.clone.sunk | while | flops 13643786 | bytes 8453379 | solution.py:72
  247.6 1.8 fusion.55
  250.5 10.8 %all-reduce.2 = (f32[1024]{0:T(1024)S(1)}, f32[1024]{0:T(1024)S(1)}, f32[]{:T(128)}) all-reduce(f32[1024]{0:T(1024)S(1)} %bitcast.83, f32[1024]{0:T(1024)S(1)} %bitcast.84, f32[]{:T(128)} %get-tuple-element.117), channel_id=1, replica_groups=mesh['grp'=4,'inner'=8] {'grp'}, use_global_device_ids=true, to_apply=%region_5.5 | all-reduce | flops 2049 | bytes 16392 | tf_op jit(solution)/shard_map/while/body/eval_jaxpr/psum | solution.py:57
  268.7 9.9 %all-reduce.2 = (f32[1024]{0:T(1024)S(1)}, f32[1024]{0:T(1024)S(1)}, f32[]{:T(128)}) all-reduce(f32[1024]{0:T(1024)S(1)} %bitcast.83, f32[1024]{0:T(1024)S(1)} %bitcast.84, f32[]{:T(128)} %get-tuple-element.117), channel_id=1, replica_groups=mesh['grp'=4,'inner'=8] {'grp'}, use_global_device_ids=true, to_apply=%region_5.5 | all-reduce | flops 2049 | bytes 16392 | tf_op jit(solution)/shard_map/while/body/eval_jaxpr/psum | solution.py:57
  285.9 10.8 %all-reduce.2 = (f32[1024]{0:T(1024)S(1)}, f32[1024]{0:T(1024)S(1)}, f32[]{:T(128)}) all-reduce(f32[1024]{0:T(1024)S(1)} %bitcast.83, f32[1024]{0:T(1024)S(1)} %bitcast.84, f32[]{:T(128)} %get-tuple-element.117), channel_id=1, replica_groups=mesh['grp'=4,'inner'=8] {'grp'}, use_global_device_ids=true, to_apply=%region_5.5 | all-reduce | flops 2049 | bytes 16392 | tf_op jit(solution)/shard_map/while/body/eval_jaxpr/psum | solution.py:57
  301.1 1.8 fusion.55
  304.0 9.9 %all-reduce.2 = (f32[1024]{0:T(1024)S(1)}, f32[1024]{0:T(1024)S(1)}, f32[]{:T(128)}) all-reduce(f32[1024]{0:T(1024)S(1)} %bitcast.83, f32[1024]{0:T(1024)S(1)} %bitcast.84, f32[]{:T(128)} %get-tuple-element.117), channel_id=1, replica_groups=mesh['grp'=4,'inner'=8] {'grp'}, use_global_device_ids=true, to_apply=%region_5.5 | all-reduce | flops 2049 | bytes 16392 | tf_op jit(solution)/shard_map/while/body/eval_jaxpr/psum | solution.py:57
  318.4 1.8 fusion.55
  321.3 10.8 %all-reduce.2 = (f32[1024]{0:T(1024)S(1)}, f32[1024]{0:T(1024)S(1)}, f32[]{:T(128)}) all-reduce(f32[1024]{0:T(1024)S(1)} %bitcast.83, f32[1024]{0:T(1024)S(1)} %bitcast.84, f32[]{:T(128)} %get-tuple-element.117), channel_id=1, replica_groups=mesh['grp'=4,'inner'=8] {'grp'}, use_global_device_ids=true, to_apply=%region_5.5 | all-reduce | flops 2049 | bytes 16392 | tf_op jit(solution)/shard_map/while/body/eval_jaxpr/psum | solution.py:57
  336.5 1.8 fusion.55
  339.4 9.9 %all-reduce.2 = (f32[1024]{0:T(1024)S(1)}, f32[1024]{0:T(1024)S(1)}, f32[]{:T(128)}) all-reduce(f32[1024]{0:T(1024)S(1)} %bitcast.83, f32[1024]{0:T(1024)S(1)} %bitcast.84, f32[]{:T(128)} %get-tuple-element.117), channel_id=1, replica_groups=mesh['grp'=4,'inner'=8] {'grp'}, use_global_device_ids=true, to_apply=%region_5.5 | all-reduce | flops 2049 | bytes 16392 | tf_op jit(solution)/shard_map/while/body/eval_jaxpr/psum | solution.py:57
  353.8 1.8 fusion.55
  356.7 10.8 %all-reduce.2 = (f32[1024]{0:T(1024)S(1)}, f32[1024]{0:T(1024)S(1)}, f32[]{:T(128)}) all-reduce(f32[1024]{0:T(1024)S(1)} %bitcast.83, f32[1024]{0:T(1024)S(1)} %bitcast.84, f32[]{:T(128)} %get-tuple-element.117), channel_id=1, replica_groups=mesh['grp'=4,'inner'=8] {'grp'}, use_global_device_ids=true, to_apply=%region_5.5 | all-reduce | flops 2049 | bytes 16392 | tf_op jit(solution)/shard_map/while/body/eval_jaxpr/psum | solution.py:57
  371.9 1.8 fusion.55
  374.8 9.9 %all-reduce.2 = (f32[1024]{0:T(1024)S(1)}, f32[1024]{0:T(1024)S(1)}, f32[]{:T(128)}) all-reduce(f32[1024]{0:T(1024)S(1)} %bitcast.83, f32[1024]{0:T(1024)S(1)} %bitcast.84, f32[]{:T(128)} %get-tuple-element.117), channel_id=1, replica_groups=mesh['grp'=4,'inner'=8] {'grp'}, use_global_device_ids=true, to_apply=%region_5.5 | all-reduce | flops 2049 | bytes 16392 | tf_op jit(solution)/shard_map/while/body/eval_jaxpr/psum | solution.py:57
  388.5 1.8 copy.27
  (97 shorter events, 33.5 us)
Async XLA Ops:
  36.9 6.5 %copy-start = (s32[1,2048]{1,0:T(1,128)S(1)}, s32[1,2048]{1,0:T(1,128)}, u32[]{:S(2)}) copy-start(s32[1,2048]{1,0:T(1,128)} %param.7) | copy-start | bytes 24580
  36.9 54.7 %all-to-all-start = ((bf16[4,2,131072]{2,1,0:T(2,128)(2,1)}), bf16[4,2,131072]{2,1,0:T(2,128)(2,1)S(1)}, u32[]{:S(2)}, u32[]{:S(2)}) async-start(bf16[4,2,131072]{2,1,0:T(2,128)(2,1)} %reshape.93), calls=%async_computation | async-start | bytes 4194304 | tf_op jit(solution)/shard_map/all_to_all | solution.py:41
  43.4 148.5 %all-reduce.5.cloned.1.call-start = ((), (), s32[]{:S(2)}) async-start(), calls=%async_computation.2 | async-start | bytes 4194304 | tf_op jit(solution)/shard_map/psum | solution.py:48
  191.9 51.6 %all-to-all-start.1 = ((f32[4,512,256]{2,1,0:T(8,128)}), f32[4,512,256]{2,1,0:T(8,128)S(1)}, u32[]{:S(2)}, u32[]{:S(2)}) async-start(f32[4,512,256]{2,1,0:T(8,128)} %all-reduce.5.cloned.1.call-done), calls=%async_computation.1 | async-start | bytes 4194304 | tf_op jit(solution)/shard_map/all_to_all | solution.py:49
Sparse Core Ops, SparseCore 0:
  131.0 60.9 all-reduce.4
where the time goes:
time: 398 us; the launch traced here: 397 us
  waiting for transfers between devices  156 us (39%)
  blocking collectives  82.7 us (21%)
  local copies, waits for them, and re-layouts  56 us (14%)
  matrix products  28 us (7%)
  other arithmetic  27.4 us (7%)
  loops' own time  22.4 us (6%)
  between operations  13.5 us (3%)
  starting transfers between devices  11 us (3%)
    psum x8, blocking collectives, reflect(): lax.psum((jnp.sum(column * column), jnp.dot(column, current, precision=hi...  82.7 us
    psum x1, waiting for transfers between devices, on_device(): summed = lax.psum(partial_value, 'inner')  61.1 us
    all_to_all x1, waiting for transfers between devices, on_device(): lax.all_to_all(second_pass, 'grp', split_axis=2, concat_axis=1, tiled=True)  48.1 us
    all_to_all x1, waiting for transfers between devices, on_device(): lax.all_to_all(summed, 'grp', split_axis=0, concat_axis=1, tiled=True)  47.1 us
    another operation x1, loops' own time, on_device(): result = lax.fori_loop(0, COLS_DONE, reflect, sketch)  22.4 us
    gather x2, local copies, waits for them, and re-layouts, pick_rows(): return jnp.take(table_rows, chosen_rows, axis=0)  21.4 us
    dot_general x8, matrix products, reflect(): jnp.dot(column, current, precision=highest)  14.5 us
    unnamed x1, other arithmetic  12.8 us
  transfers between devices with their start and end apart: 3, of which 3 were waited for; matrix products, arithmetic and copies ran while one was open for 0% of the time, Pallas kernels for 0%

commit v1 on v0

--- a/solution.py
+++ b/solution.py
@@ -38,7 +38,12 @@
         "hb,mbcd->mhcd", hadamard, middle_view, preferred_element_type=jnp.float32
     ).astype(jnp.bfloat16)
     second_pass = second_pass.reshape(block_count, local_rows, columns)
-    gathered_rows = lax.all_to_all(second_pass, "grp", split_axis=2, concat_axis=1, tiled=True)
+    gathered_rows = jnp.concatenate(
+        lax.all_to_all(
+            jnp.stack(jnp.split(second_pass, lax.axis_size("grp"), axis=2)), "grp", 0, 0
+        ),
+        axis=1,
+    )
     col_count = gathered_rows.shape[2]
     by_piece = gathered_rows.reshape(block_count, 16, 256, col_count)
     mixed_rows = jnp.einsum("ha,nakd->nhkd", hadamard, by_piece, preferred_element_type=jnp.float32)

time: 398 us -> 363 us (0.912)
  local copies, waits for them, and re-layouts: 56 us -> 35.5 us
  other arithmetic: 27.4 us -> 16.2 us
    unnamed x1 -> x0, other arithmetic: 12.8 us -> none
    unnamed x6 -> x2, local copies, waits for them, and re-layouts: 9.63 us -> 0.01 us
    reshape x1 -> x0, local copies, waits for them, and re-layouts: 7.75 us -> none  [on_device(): second_pass = second_pass.reshape(block_count, local_rows, columns)]
where the time goes in v1:
time: 363 us; the launch traced here: 362 us
  waiting for transfers between devices  156 us (43%)
  blocking collectives  82.8 us (23%)
  local copies, waits for them, and re-layouts  35.5 us (10%)
  matrix products  26.4 us (7%)
  loops' own time  20.3 us (6%)
  other arithmetic  16.2 us (4%)
  between operations  13.5 us (4%)
  starting transfers between devices  11 us (3%)
    psum x8, blocking collectives, reflect(): lax.psum((jnp.sum(column * column), jnp.dot(column, current, precision=hi...  82.8 us
    psum x1, waiting for transfers between devices, on_device(): summed = lax.psum(partial_value, 'inner')  61 us
    all_to_all x1, waiting for transfers between devices, on_device(): lax.all_to_all(jnp.stack(jnp.split(second_pass, lax.axis_size('grp'), axi...  48.1 us
    all_to_all x1, waiting for transfers between devices, on_device(): lax.all_to_all(summed, 'grp', split_axis=0, concat_axis=1, tiled=True)  47.1 us
    gather x2, local copies, waits for them, and re-layouts, pick_rows(): return jnp.take(table_rows, chosen_rows, axis=0)  21.4 us
    another operation x1, loops' own time, on_device(): result = lax.fori_loop(0, COLS_DONE, reflect, sketch)  20.3 us
    dot_general x8, matrix products, reflect(): jnp.dot(column, current, precision=highest)  14.5 us
    dot_general x8, matrix products, reflect(): jnp.dot(is_pivot, current, precision=highest)  8.36 us
  transfers between devices with their start and end apart: 3, of which 3 were waited for; matrix products, arithmetic and copies ran while one was open for 0% of the time, Pallas kernels for 0%

profile of v1, /device:TPU:0, one launch (start us, length us, event | category | flops | bytes accessed | tf_op | source)
XLA Modules:
  0.0 361.9 jit_solution(16937396548421528979)
XLA Ops:
  7.2 2.5 multiply_convert_fusion
  10.4 1.5 convert_bitcast_fusion
  13.3 1.6 pad_maximum_fusion
  14.8 6.5 %all-to-all-start = ((bf16[4,1,1024,256]{3,2,1,0:T(8,128)(2,1)}), bf16[4,1,1024,256]{3,2,1,0:T(8,128)(2,1)S(1)}, u32[]{:S(2)}, u32[]{:S(2)}) async-start(bf16[4,1,1024,256]{3,2,1,0:T(8,128)(2,1)} %pad_maximum_fusion), calls=%async_computation | async-start | bytes 4194304 | tf_op jit(solution)/shard_map/all_to_all | solution.py:42
  21.4 48.1 %all-to-all-done = bf16[4,1,1024,256]{3,2,1,0:T(8,128)(2,1)S(1)} async-done(((bf16[4,1,1024,256]{3,2,1,0:T(8,128)(2,1)}), bf16[4,1,1024,256]{3,2,1,0:T(8,128)(2,1)S(1)}, u32[]{:S(2)}, u32[]{:S(2)}) %all-to-all-start) | async-done | bytes 2097184 | tf_op jit(solution)/shard_map/all_to_all | solution.py:42
  69.5 1.3 convolution_bitcast_fusion
  70.9 4.4 %copy.9 = f32[1,16,256,256]{3,2,1,0:T(8,128)} copy(f32[1,16,256,256]{3,1,2,0:T(8,128)S(1)} %convolution_bitcast_fusion) | data formatting | bytes 8388608 | tf_op jit(solution)/shard_map/ha,nakd->nhkd/transpose | solution.py:49
  75.2 21.4 %gather_fusion = f32[2048,256]{1,0:T(8,128)S(1)} fusion(f32[1,4096,256]{2,1,0:T(8,128)} %bitcast.77, s32[2048]{0:T(1024)S(1)} %bitcast.76), kind=kCustom, calls=%fused_computation | custom fusion | bytes 4210688 | tf_op jit(solution)/shard_map/vmap(jit(_take))/gather | solution.py:20
  96.6 1.7 broadcast_select_fusion.2
  98.3 61.0 %all-reduce.5.cloned.1.call-done = f32[4,512,256]{2,1,0:T(8,128)} async-done(((f32[4,512,256]{2,1,0:T(8,128)}), f32[4,512,256]{2,1,0:T(8,128)}) %all-reduce.5.cloned.1.call-update) | async-done | bytes 2097168 | tf_op jit(solution)/shard_map/psum | solution.py:53
  159.3 4.5 %all-to-all-start.1 = ((f32[4,512,256]{2,1,0:T(8,128)}), f32[4,512,256]{2,1,0:T(8,128)S(1)}, u32[]{:S(2)}, u32[]{:S(2)}) async-start(f32[4,512,256]{2,1,0:T(8,128)} %all-reduce.5.cloned.1.call-done), calls=%async_computation.1 | async-start | bytes 4194304 | tf_op jit(solution)/shard_map/all_to_all | solution.py:54
  163.8 47.1 %all-to-all-done.1 = f32[4,512,256]{2,1,0:T(8,128)S(1)} async-done(((f32[4,512,256]{2,1,0:T(8,128)}), f32[4,512,256]{2,1,0:T(8,128)S(1)}, u32[]{:S(2)}, u32[]{:S(2)}) %all-to-all-start.1) | async-done | bytes 2097184 | tf_op jit(solution)/shard_map/all_to_all | solution.py:54
  211.0 1.5 multiply_bitcast_fusion
  212.5 1.9 copy.10
  214.4 138.8 %while.14 = (s32[]{:T(128)}, f32[512,1024]{0,1:T(8,128)S(1)}, s32[]{:T(128)}, s32[]{:T(128)}, f32[]{:T(128)}, /*index=5*/f32[]{:T(128)}, f32[]{:T(128)}, f32[]{:T(128)}, f32[]{:T(128)}) while((s32[]{:T(128)}, f32[512,1024]{0,1:T(8,128)S(1)}, s32[]{:T(128)}, s32[]{:T(128)}, f32[]{:T(128)}, /*index=5*/f32[]{:T(128)}, f32[]{:T(128)}, ...), condition=%wide.region_6.7_spmd.clone, body=%wide.region_1.6_spmd.clone.sunk | while | flops 13643786 | bytes 8453379 | solution.py:77
  215.0 1.8 fusion.55
  217.9 10.8 %all-reduce.2 = (f32[1024]{0:T(1024)S(1)}, f32[1024]{0:T(1024)S(1)}, f32[]{:T(128)}) all-reduce(f32[1024]{0:T(1024)S(1)} %bitcast.83, f32[1024]{0:T(1024)S(1)} %bitcast.84, f32[]{:T(128)} %get-tuple-element.121), channel_id=1, replica_groups=mesh['grp'=4,'inner'=8] {'grp'}, use_global_device_ids=true, to_apply=%region_5.5 | all-reduce | flops 2049 | bytes 16392 | tf_op jit(solution)/shard_map/while/body/eval_jaxpr/psum | solution.py:62
  232.8 1.8 fusion.55
  235.7 9.9 %all-reduce.2 = (f32[1024]{0:T(1024)S(1)}, f32[1024]{0:T(1024)S(1)}, f32[]{:T(128)}) all-reduce(f32[1024]{0:T(1024)S(1)} %bitcast.83, f32[1024]{0:T(1024)S(1)} %bitcast.84, f32[]{:T(128)} %get-tuple-element.121), channel_id=1, replica_groups=mesh['grp'=4,'inner'=8] {'grp'}, use_global_device_ids=true, to_apply=%region_5.5 | all-reduce | flops 2049 | bytes 16392 | tf_op jit(solution)/shard_map/while/body/eval_jaxpr/psum | solution.py:62
  249.7 1.8 fusion.55
  252.6 10.8 %all-reduce.2 = (f32[1024]{0:T(1024)S(1)}, f32[1024]{0:T(1024)S(1)}, f32[]{:T(128)}) all-reduce(f32[1024]{0:T(1024)S(1)} %bitcast.83, f32[1024]{0:T(1024)S(1)} %bitcast.84, f32[]{:T(128)} %get-tuple-element.121), channel_id=1, replica_groups=mesh['grp'=4,'inner'=8] {'grp'}, use_global_device_ids=true, to_apply=%region_5.5 | all-reduce | flops 2049 | bytes 16392 | tf_op jit(solution)/shard_map/while/body/eval_jaxpr/psum | solution.py:62
  267.5 1.8 fusion.55
  270.4 9.9 %all-reduce.2 = (f32[1024]{0:T(1024)S(1)}, f32[1024]{0:T(1024)S(1)}, f32[]{:T(128)}) all-reduce(f32[1024]{0:T(1024)S(1)} %bitcast.83, f32[1024]{0:T(1024)S(1)} %bitcast.84, f32[]{:T(128)} %get-tuple-element.121), channel_id=1, replica_groups=mesh['grp'=4,'inner'=8] {'grp'}, use_global_device_ids=true, to_apply=%region_5.5 | all-reduce | flops 2049 | bytes 16392 | tf_op jit(solution)/shard_map/while/body/eval_jaxpr/psum | solution.py:62
  284.4 1.8 fusion.55
  287.3 10.8 %all-reduce.2 = (f32[1024]{0:T(1024)S(1)}, f32[1024]{0:T(1024)S(1)}, f32[]{:T(128)}) all-reduce(f32[1024]{0:T(1024)S(1)} %bitcast.83, f32[1024]{0:T(1024)S(1)} %bitcast.84, f32[]{:T(128)} %get-tuple-element.121), channel_id=1, replica_groups=mesh['grp'=4,'inner'=8] {'grp'}, use_global_device_ids=true, to_apply=%region_5.5 | all-reduce | flops 2049 | bytes 16392 | tf_op jit(solution)/shard_map/while/body/eval_jaxpr/psum | solution.py:62
  302.2 1.8 fusion.55
  305.1 9.9 %all-reduce.2 = (f32[1024]{0:T(1024)S(1)}, f32[1024]{0:T(1024)S(1)}, f32[]{:T(128)}) all-reduce(f32[1024]{0:T(1024)S(1)} %bitcast.83, f32[1024]{0:T(1024)S(1)} %bitcast.84, f32[]{:T(128)} %get-tuple-element.121), channel_id=1, replica_groups=mesh['grp'=4,'inner'=8] {'grp'}, use_global_device_ids=true, to_apply=%region_5.5 | all-reduce | flops 2049 | bytes 16392 | tf_op jit(solution)/shard_map/while/body/eval_jaxpr/psum | solution.py:62
  319.1 1.8 fusion.55
  322.0 10.8 %all-reduce.2 = (f32[1024]{0:T(1024)S(1)}, f32[1024]{0:T(1024)S(1)}, f32[]{:T(128)}) all-reduce(f32[1024]{0:T(1024)S(1)} %bitcast.83, f32[1024]{0:T(1024)S(1)} %bitcast.84, f32[]{:T(128)} %get-tuple-element.121), channel_id=1, replica_groups=mesh['grp'=4,'inner'=8] {'grp'}, use_global_device_ids=true, to_apply=%region_5.5 | all-reduce | flops 2049 | bytes 16392 | tf_op jit(solution)/shard_map/while/body/eval_jaxpr/psum | solution.py:62
  336.9 1.8 fusion.55
  339.8 9.9 %all-reduce.2 = (f32[1024]{0:T(1024)S(1)}, f32[1024]{0:T(1024)S(1)}, f32[]{:T(128)}) all-reduce(f32[1024]{0:T(1024)S(1)} %bitcast.83, f32[1024]{0:T(1024)S(1)} %bitcast.84, f32[]{:T(128)} %get-tuple-element.121), channel_id=1, replica_groups=mesh['grp'=4,'inner'=8] {'grp'}, use_global_device_ids=true, to_apply=%region_5.5 | all-reduce | flops 2049 | bytes 16392 | tf_op jit(solution)/shard_map/while/body/eval_jaxpr/psum | solution.py:62
  353.3 1.8 copy.11
  (92 shorter events, 24.1 us)
Async XLA Ops:
  14.8 6.5 %copy-start = (s32[1,2048]{1,0:T(1,128)S(1)}, s32[1,2048]{1,0:T(1,128)}, u32[]{:S(2)}) copy-start(s32[1,2048]{1,0:T(1,128)} %param.7) | copy-start | bytes 24580
  14.8 54.7 %all-to-all-start = ((bf16[4,1,1024,256]{3,2,1,0:T(8,128)(2,1)}), bf16[4,1,1024,256]{3,2,1,0:T(8,128)(2,1)S(1)}, u32[]{:S(2)}, u32[]{:S(2)}) async-start(bf16[4,1,1024,256]{3,2,1,0:T(8,128)(2,1)} %pad_maximum_fusion), calls=%async_computation | async-start | bytes 4194304 | tf_op jit(solution)/shard_map/all_to_all | solution.py:42
  21.3 138.0 %all-reduce.5.cloned.1.call-start = ((), (), s32[]{:S(2)}) async-start(), calls=%async_computation.2 | async-start | bytes 4194304 | tf_op jit(solution)/shard_map/psum | solution.py:53
  159.3 51.6 %all-to-all-start.1 = ((f32[4,512,256]{2,1,0:T(8,128)}), f32[4,512,256]{2,1,0:T(8,128)S(1)}, u32[]{:S(2)}, u32[]{:S(2)}) async-start(f32[4,512,256]{2,1,0:T(8,128)} %all-reduce.5.cloned.1.call-done), calls=%async_computation.1 | async-start | bytes 4194304 | tf_op jit(solution)/shard_map/all_to_all | solution.py:54
Sparse Core Ops, SparseCore 0:
  98.4 60.8 all-reduce.4
